TPU v7x, 32 devices: a whole 2x2x4 slice. The times are simulated.
32 devices in a mesh: sub: 8 (over z, x), blk: 4 (over y, core).
Axes of the slice: x: 2, y: 2, z: 4, core: 2. Of those that a mesh axis runs over, the one named last changes fastest.
Arguments:
- a_tiles: bfloat16 [768, 12, 128, 128], P(('sub', 'blk'))
- modes: bfloat16 [768, 16, 128], P(('sub', 'blk')), may hold values from -6 to 6
- col_tiles: int32 [768, 12], P(('sub', 'blk')), may hold values from 0 to 221, as said below
- fetch_list: int32 [32, 126], P(('sub', 'blk')), may hold values from 0 to 767, as said below
Outputs:
- prolong: bfloat16 [768, 12, 16, 128], P(('sub', 'blk'))
- coarse_diag: float32 [768, 256], P('sub')
Inputs may be any that keep to these rules, and one draw needn't show every extreme that they name: `col_tiles`: slot 0 of row tile t names t itself (its index within its group); the other slots name other tiles of the same group (values below 96) or 96 + h for entry h of the device's fetch list; every entry of a device's fetch list is named by some slot of that device's rows. `fetch_list`: A device's list is 7 blocks of 18 entries; each block names distinct tiles of one group other than the device's own, different blocks name different groups; tile i of group g has number g * 96 + i.
All inputs are finite; a program needn't handle non-finite values.
Results may differ from a plain program's by a relative error of at most 0.008.
Values may be sent and summed in bfloat16 or wider, within the bound.
No kernel may reach another device: no remote copies, remote signals or barrier semaphores. Data moves between devices by JAX's collectives and lax.ppermute only.
A program may use at most 64 MiB of HBM per device.

v0:
```python
import jax
import jax.numpy as jnp
from jax import lax
from jax.sharding import PartitionSpec as P

NEIGHBOURS = 26
damping = 2.0 / 3.0


def shards(a_tiles, modes, col_tiles, fetch_list):
    blk_count = lax.axis_size("blk")
    sub_count = lax.axis_size("sub")
    tile_dev = a_tiles.shape[0]
    slot_count = a_tiles.shape[1]
    tile_rows = a_tiles.shape[2]
    mode_count = modes.shape[1]
    group_size = tile_dev * blk_count
    ghost_count = fetch_list.shape[1]
    peer_count = min(NEIGHBOURS, sub_count - 1)
    per_peer = ghost_count // peer_count
    group_modes = lax.all_gather(modes, "blk", axis=0, tiled=True)
    wanted = fetch_list[0].reshape(peer_count, per_peer)
    owners = wanted[:, 0] // group_size
    within = wanted % group_size
    selector = (owners[:, None] == jnp.arange(sub_count, dtype=jnp.int32)[None, :]).astype(
        jnp.int32
    )
    requests = jnp.sum(selector[:, :, None] * (within + 1)[:, None, :], axis=0)
    received = lax.all_to_all(requests, "sub", split_axis=0, concat_axis=0, tiled=True)
    present = received > 0
    picked = group_modes[jnp.maximum(received - 1, 0)]
    picked = jnp.where(present[:, :, None, None], picked, jnp.zeros_like(picked))
    returned = lax.all_to_all(picked, "sub", split_axis=0, concat_axis=0, tiled=True)
    returned, received = (returned, received)
    ghosts = returned[owners].reshape(ghost_count, mode_count, tile_rows)
    lookup = jnp.concatenate([group_modes, ghosts], axis=0)
    gathered = lookup[col_tiles]
    product = jnp.einsum("tkrc,tkmc->tkmr", a_tiles, gathered, preferred_element_type=jnp.float32)
    inverse = 1.0 / jnp.diagonal(a_tiles[:, 0], axis1=1, axis2=2).astype(jnp.float32)
    leading = (jnp.arange(slot_count) == 0).astype(jnp.float32)
    prolong = (
        leading[None, :, None, None] * modes.astype(jnp.float32)[:, None]
        - damping * inverse[:, None, None, :] * product
    ).astype(jnp.bfloat16)
    partial_value = (
        jnp.einsum(
            "tkmr,tknr->tkmn", prolong.astype(jnp.float32), product, precision=lax.Precision.HIGHEST
        )
        / tile_rows
    )
    partial_value = partial_value.reshape(tile_dev * slot_count, mode_count * mode_count)
    segment = (
        col_tiles.reshape(-1)[:, None]
        == jnp.arange(group_size + ghost_count, dtype=jnp.int32)[None, :]
    ).astype(jnp.float32)
    slot_sums = jnp.dot(
        segment.T,
        partial_value,
        precision=lax.Precision.HIGHEST,
        preferred_element_type=jnp.float32,
    )
    ghost_sums = slot_sums[group_size:].reshape(peer_count, per_peer, mode_count * mode_count)
    outgoing = jnp.einsum(
        "jp,jmv->pmv", selector.astype(jnp.float32), ghost_sums, precision=lax.Precision.HIGHEST
    )
    incoming = lax.all_to_all(
        outgoing.astype(jnp.bfloat16), "sub", split_axis=0, concat_axis=0, tiled=True
    ).astype(outgoing.dtype)
    target = (
        received[:, :, None] == jnp.arange(1, group_size + 1, dtype=jnp.int32)[None, None, :]
    ).astype(jnp.float32)
    local_sum = slot_sums[:group_size] + jnp.einsum(
        "pmg,pmv->gv", target, incoming, precision=lax.Precision.HIGHEST
    )
    coarse_diag = lax.psum(local_sum.astype(jnp.bfloat16), "blk").astype(jnp.float32)
    return (prolong, coarse_diag)


def solution(mesh):
    in_specs = (
        P(("sub", "blk"), None, None, None),
        P(("sub", "blk"), None, None),
        P(("sub", "blk"), None),
        P(("sub", "blk"), None),
    )
    out_specs = (P(("sub", "blk"), None, None, None), P("sub", None))
    return jax.shard_map(shards, mesh=mesh, in_specs=in_specs, out_specs=out_specs, check_vma=False)
```

profile of v0, /device:TPU:0, one launch (start us, length us, event | category | flops | bytes accessed | tf_op | source)
XLA Modules:
  0.0 80.3 jit_solution(5689057946343639641)
XLA Ops:
  0.6 0.5 broadcast.175
  1.2 1.3 %reduce.11 = s32[126]{0:T(128)S(1)} reduce(s32[1,126]{1,0:T(1,128)} %param.7, s32[]{:T(128)} %broadcast.175), dimensions={0}, to_apply=%param.7.reduce_sub_computation.3 | reduce | bytes 1012 | tf_op args[3]
  2.8 0.7 multiply_reduce_fusion
  3.5 7.3 %all-to-all-start = ((s32[8,1,18]{2,1,0:T(1,128)}), s32[8,1,18]{2,1,0:T(1,128)S(1)}, u32[]{:S(2)}, u32[]{:S(2)}) async-start(s32[8,1,18]{2,1,0:T(1,128)} %bitcast.4), calls=%async_computation | async-start | bytes 8192 | tf_op jit(solution)/shard_map/all_to_all | solution.py:29
  10.8 6.7 %all_gather.3 = bf16[96,16,128]{2,1,0:T(8,128)(2,1)S(1)} all-gather(bf16[24,16,128]{2,1,0:T(8,128)(2,1)} %param.5), channel_id=1, replica_groups=mesh['sub'=8,'blk'=4] {'blk'}, dimensions={0}, use_global_device_ids=true | all-gather | bytes 491520 | tf_op jit(solution)/shard_map/all_gather | solution.py:21
  17.6 0.7 gather_fusion.1
  18.3 1.0 %broadcast_select_fusion = bf16[8,18,16,128]{3,2,1,0:T(8,128)(2,1)} fusion(bf16[8,18,16,128]{3,2,1,0:T(8,128)(2,1)S(1)} %bitcast.31, pred[8,18]{1,0:T(8,128)(4,1)S(1)} %broadcast_compare_fusion), kind=kLoop, calls=%fused_computation.11 | loop fusion | flops 294912 | bytes 1179792 | tf_op jit(solution)/shard_map/jit(_where)/select_n | solution.py:32
  19.4 6.0 %all-to-all-start.1 = ((bf16[8,18,16,128]{3,2,1,0:T(8,128)(2,1)}), bf16[8,18,16,128]{3,2,1,0:T(8,128)(2,1)S(1)}, u32[]{:S(2)}, u32[]{:S(2)}) async-start(bf16[8,18,16,128]{3,2,1,0:T(8,128)(2,1)} %broadcast_select_fusion), calls=%async_computation.1 | async-start | bytes 1179648 | tf_op jit(solution)/shard_map/all_to_all | solution.py:33
  25.4 3.2 %copy.42 = bf16[24,1,128,128]{0,3,2,1:T(8,128)(2,1)} copy(bf16[24,1,128,128]{3,2,1,0:T(8,128)(2,1)S(1)} %slice-done) | data formatting | bytes 1572864
  28.6 1.9 %gather_fusion = bf16[128,24]{1,0:T(8,128)(2,1)S(1)} fusion(bf16[24,128,128]{0,2,1:T(8,128)(2,1)} %bitcast.30, s32[128]{0:T(128)S(1)} %or_bitcast_fusion), kind=kCustom, calls=%fused_computation | custom fusion | bytes 13312 | tf_op jit(solution)/shard_map/jit(diagonal)/gather | solution.py:39
  31.1 10.7 %all-to-all-done.1 = bf16[8,18,16,128]{3,2,1,0:T(8,128)(2,1)S(1)} async-done(((bf16[8,18,16,128]{3,2,1,0:T(8,128)(2,1)}), bf16[8,18,16,128]{3,2,1,0:T(8,128)(2,1)S(1)}, u32[]{:S(2)}, u32[]{:S(2)}) %all-to-all-start.1) | async-done | bytes 589856 | tf_op jit(solution)/shard_map/all_to_all | solution.py:33
  41.8 0.6 gather_fusion.2
  42.5 1.8 %gather_fusion.3 = bf16[288,16,128]{2,1,0:T(8,128)(2,1)S(1)} fusion(bf16[222,16,128]{2,1,0:T(8,128)(2,1)S(1)} %pad_maximum_fusion, s32[1024]{0:T(1024)S(1)} %pad_clamp_fusion), kind=kCustom, calls=%fused_computation.3 | custom fusion | bytes 2360448 | tf_op jit(solution)/shard_map/gather | solution.py:37
  44.4 7.5 %subtract_convert_fusion = (bf16[24,12,16,128]{3,2,1,0:T(8,128)(2,1)S(1)}, f32[24,12,16,128]{3,2,1,0:T(8,128)S(1)}) fusion(f32[24,128]{1,0:T(8,128)S(1)} %multiply_bitcast_fusion, f32[24,16,128]{2,1,0:T(8,128)S(1)} %convert_element_type.44, f32[12]{0:T(128)S(1)} %compare_convert_fusion, bf16[24,12,16,128]{3,2,1,0:T(8,128)(2,1)S(1)} %bitcast.29, ...), kind=kOutput, calls=%fused_computation.4 | convolution fusion | flops 153354240 | bytes 14364720 | tf_op jit(solution)/shard_map/tkrc,tkmc->tkmr/dot_general | solution.py:38
  51.8 2.0 %convolution_multiply_fusion = f32[24,12,16,16]{3,2,1,0:T(8,128)S(1)} fusion(bf16[24,12,16,128]{3,2,1,0:T(8,128)(2,1)S(1)} %get-tuple-element.4, f32[24,12,16,128]{3,2,1,0:T(8,128)S(1)} %get-tuple-element.5), kind=kOutput, calls=%fused_computation.5 | convolution fusion | flops 113319936 | bytes 3833856 | tf_op jit(solution)/shard_map/tkmr,tknr->tkmn/dot_general | solution.py:46
  53.8 1.7 %reshape.91 = f32[288,256]{1,0:T(8,128)} reshape(f32[24,12,16,16]{3,2,1,0:T(8,128)S(1)} %convolution_multiply_fusion) | data formatting | bytes 589824 | tf_op jit(solution)/shard_map/reshape | solution.py:51
  55.5 1.5 %fusion.2 = f32[222,256]{1,0:T(8,128)S(1)} fusion(f32[288,256]{1,0:T(8,128)} %reshape.91, s32[288]{0:T(512)S(1)} %eq.58), kind=kOutput, calls=%fused_computation.13 | convolution fusion | flops 196475328 | bytes 523392 | tf_op jit(solution)/shard_map/dot_general | solution.py:56
  57.1 0.3 convolution_convert_fusion
  57.4 0.7 copy.41
  58.0 3.6 %all-to-all-start.2 = ((bf16[8,18,256]{2,1,0:T(8,128)(2,1)}), bf16[8,18,256]{2,1,0:T(8,128)(2,1)S(1)}, u32[]{:S(2)}, u32[]{:S(2)}) async-start(bf16[8,18,256]{2,1,0:T(8,128)(2,1)} %copy.41), calls=%async_computation.2 | async-start | bytes 196608 | tf_op jit(solution)/shard_map/all_to_all | solution.py:66
  61.7 7.1 %all-to-all-done.2 = bf16[8,18,256]{2,1,0:T(8,128)(2,1)S(1)} async-done(((bf16[8,18,256]{2,1,0:T(8,128)(2,1)}), bf16[8,18,256]{2,1,0:T(8,128)(2,1)S(1)}, u32[]{:S(2)}, u32[]{:S(2)}) %all-to-all-start.2) | async-done | bytes 73760 | tf_op jit(solution)/shard_map/all_to_all | solution.py:66
  68.8 0.3 fusion.1
  69.1 10.5 %psum.7 = bf16[96,256]{1,0:T(8,128)(2,1)S(1)} all-reduce(bf16[96,256]{1,0:T(8,128)(2,1)S(1)} %fusion.1), channel_id=1, replica_groups=mesh['sub'=8,'blk'=4] {'blk'}, use_global_device_ids=true, to_apply=%region_1.2 | all-reduce | flops 24576 | bytes 98304 | tf_op jit(solution)/shard_map/psum | solution.py:75
  79.6 0.6 convert_element_type.51
  (34 shorter events, 1.1 us)
Async XLA Ops:
  0.6 24.7 %copy-start.1 = (bf16[24,16,128]{2,1,0:T(8,128)(2,1)S(1)}, bf16[24,16,128]{2,1,0:T(8,128)(2,1)}, u32[]{:S(2)}) copy-start(bf16[24,16,128]{2,1,0:T(8,128)(2,1)} %param.5) | copy-start | bytes 294916
  3.5 14.0 %all-to-all-start = ((s32[8,1,18]{2,1,0:T(1,128)}), s32[8,1,18]{2,1,0:T(1,128)S(1)}, u32[]{:S(2)}, u32[]{:S(2)}) async-start(s32[8,1,18]{2,1,0:T(1,128)} %bitcast.4), calls=%async_computation | async-start | bytes 8192 | tf_op jit(solution)/shard_map/all_to_all | solution.py:29
  18.3 7.1 %slice-start = ((bf16[24,12,128,128]{3,2,1,0:T(8,128)(2,1)}), bf16[24,1,128,128]{3,2,1,0:T(8,128)(2,1)S(1)}, s32[]{:S(2)}) async-start(bf16[24,12,128,128]{3,2,1,0:T(8,128)(2,1)} %param.4), calls=%async_computation.3 | async-start | bytes 1572864 | tf_op jit(solution)/shard_map/slice | solution.py:39
  19.4 22.4 %all-to-all-start.1 = ((bf16[8,18,16,128]{3,2,1,0:T(8,128)(2,1)}), bf16[8,18,16,128]{3,2,1,0:T(8,128)(2,1)S(1)}, u32[]{:S(2)}, u32[]{:S(2)}) async-start(bf16[8,18,16,128]{3,2,1,0:T(8,128)(2,1)} %broadcast_select_fusion), calls=%async_computation.1 | async-start | bytes 1179648 | tf_op jit(solution)/shard_map/all_to_all | solution.py:33
  25.4 5.3 %copy-start.2 = (s32[24,12]{0,1:T(8,128)S(1)}, s32[24,12]{0,1:T(8,128)}, u32[]{:S(2)}) copy-start(s32[24,12]{0,1:T(8,128)} %param.6) | copy-start | bytes 3460
  51.8 2.0 %copy-start = (bf16[24,12,16,128]{3,2,1,0:T(8,128)(2,1)}, bf16[24,12,16,128]{3,2,1,0:T(8,128)(2,1)S(1)}, u32[]{:S(2)}) copy-start(bf16[24,12,16,128]{3,2,1,0:T(8,128)(2,1)S(1)} %get-tuple-element.4) | copy-start | bytes 3538948
  58.0 10.8 %all-to-all-start.2 = ((bf16[8,18,256]{2,1,0:T(8,128)(2,1)}), bf16[8,18,256]{2,1,0:T(8,128)(2,1)S(1)}, u32[]{:S(2)}, u32[]{:S(2)}) async-start(bf16[8,18,256]{2,1,0:T(8,128)(2,1)} %copy.41), calls=%async_computation.2 | async-start | bytes 196608 | tf_op jit(solution)/shard_map/all_to_all | solution.py:66
where the time goes:
time: 80.7 us; the launch traced here: 80.3 us
  waiting for transfers between devices  17.8 us (22%)
  blocking collectives  17.2 us (21%)
  starting transfers between devices  16.9 us (21%)
  local copies, waits for them, and re-layouts  12 us (15%)
  matrix products  11.6 us (14%)
  other arithmetic  4.03 us (5%)
  between operations  0.83 us (1%)
    all_to_all x1, waiting for transfers between devices, shards(): lax.all_to_all(picked, 'sub', split_axis=0, concat_axis=0, tiled=True)  10.7 us
    psum x1, blocking collectives, shards(): lax.psum(local_sum.astype(jnp.bfloat16), 'blk').astype(jnp.float32)  10.5 us
    dot_general x1, matrix products, shards(): jnp.einsum('tkrc,tkmc->tkmr', a_tiles, gathered, preferred_element_type=j...  7.47 us
    all_to_all x1, starting transfers between devices, shards(): lax.all_to_all(requests, 'sub', split_axis=0, concat_axis=0, tiled=True)  7.28 us
    all_to_all x1, waiting for transfers between devices, shards(): lax.all_to_all(outgoing.astype(jnp.bfloat16), 'sub', split_axis=0, concat...  7.12 us
    all_gather x1, blocking collectives, shards(): group_modes = lax.all_gather(modes, 'blk', axis=0, tiled=True)  6.68 us
    all_to_all x1, starting transfers between devices, shards(): lax.all_to_all(picked, 'sub', split_axis=0, concat_axis=0, tiled=True)  5.99 us
    unnamed x9, local copies, waits for them, and re-layouts  3.84 us
  transfers between devices with their start and end apart: 3, of which 2 were waited for; matrix products, arithmetic and copies ran while one was open for 7% of the time, Pallas kernels for 0%

commit v1 on v0

--- a/solution.py
+++ b/solution.py
@@ -5,6 +5,11 @@
 
 NEIGHBOURS = 26
 damping = 2.0 / 3.0
+
+
+def summed_here(x, axis):
+    parts = lax.all_gather(x, axis)
+    return jnp.sum(parts, axis=0)
 
 
 def shards(a_tiles, modes, col_tiles, fetch_list):
@@ -72,7 +77,7 @@
     local_sum = slot_sums[:group_size] + jnp.einsum(
         "pmg,pmv->gv", target, incoming, precision=lax.Precision.HIGHEST
     )
-    coarse_diag = lax.psum(local_sum.astype(jnp.bfloat16), "blk").astype(jnp.float32)
+    coarse_diag = summed_here(local_sum.astype(jnp.bfloat16), "blk").astype(jnp.float32)
     return (prolong, coarse_diag)
 
 

time: 80.7 us -> 75.8 us (0.939)
  blocking collectives: 17.2 us -> 12.3 us
    psum x1 -> x0, blocking collectives: 10.5 us -> none  [shards(): lax.psum(local_sum.astype(jnp.bfloat16), 'blk').astype(jnp.float32)]
    all_gather x0 -> x1, blocking collectives: none -> 5.6 us  [summed_here(): parts = lax.all_gather(x, axis)]
  transfers between devices with their start and end apart: 3 -> 3, of which waited for: 2 -> 2; matrix products, arithmetic and copies ran while one was open for 7% -> 8% of each run, Pallas kernels for 0% -> 0%
where the time goes in v1:
time: 75.8 us; the launch traced here: 75.4 us
  waiting for transfers between devices  17.8 us (23%)
  starting transfers between devices  16.9 us (22%)
  blocking collectives  12.3 us (16%)
  local copies, waits for them, and re-layouts  12 us (16%)
  matrix products  11.6 us (15%)
  other arithmetic  4.06 us (5%)
  between operations  0.82 us (1%)
    all_to_all x1, waiting for transfers between devices, shards(): lax.all_to_all(picked, 'sub', split_axis=0, concat_axis=0, tiled=True)  10.7 us
    dot_general x1, matrix products, shards(): jnp.einsum('tkrc,tkmc->tkmr', a_tiles, gathered, preferred_element_type=j...  7.47 us
    all_to_all x1, starting transfers between devices, shards(): lax.all_to_all(requests, 'sub', split_axis=0, concat_axis=0, tiled=True)  7.28 us
    all_to_all x1, waiting for transfers between devices, shards(): lax.all_to_all(outgoing.astype(jnp.bfloat16), 'sub', split_axis=0, concat...  7.12 us
    all_gather x1, blocking collectives, shards(): group_modes = lax.all_gather(modes, 'blk', axis=0, tiled=True)  6.68 us
    all_to_all x1, starting transfers between devices, shards(): lax.all_to_all(picked, 'sub', split_axis=0, concat_axis=0, tiled=True)  5.99 us
    all_gather x1, blocking collectives, summed_here(): parts = lax.all_gather(x, axis)  5.6 us
    unnamed x9, local copies, waits for them, and re-layouts  3.84 us
  transfers between devices with their start and end apart: 3, of which 2 were waited for; matrix products, arithmetic and copies ran while one was open for 8% of the time, Pallas kernels for 0%

profile of v1, /device:TPU:0, one launch (start us, length us, event | category | flops | bytes accessed | tf_op | source)
XLA Modules:
  0.0 75.4 jit_solution(9529276588902708508)
XLA Ops:
  0.6 0.5 broadcast.175
  1.2 1.3 %reduce.12 = s32[126]{0:T(128)S(1)} reduce(s32[1,126]{1,0:T(1,128)} %param.7, s32[]{:T(128)} %broadcast.175), dimensions={0}, to_apply=%param.7.reduce_sub_computation.3 | reduce | bytes 1012 | tf_op args[3]
  2.8 0.7 multiply_reduce_fusion
  3.5 7.3 %all-to-all-start = ((s32[8,1,18]{2,1,0:T(1,128)}), s32[8,1,18]{2,1,0:T(1,128)S(1)}, u32[]{:S(2)}, u32[]{:S(2)}) async-start(s32[8,1,18]{2,1,0:T(1,128)} %bitcast.4), calls=%async_computation | async-start | bytes 8192 | tf_op jit(solution)/shard_map/all_to_all | solution.py:34
  10.8 6.7 %all_gather.9 = bf16[96,16,128]{2,1,0:T(8,128)(2,1)S(1)} all-gather(bf16[24,16,128]{2,1,0:T(8,128)(2,1)} %param.5), channel_id=1, replica_groups=mesh['sub'=8,'blk'=4] {'blk'}, dimensions={0}, use_global_device_ids=true | all-gather | bytes 491520 | tf_op jit(solution)/shard_map/all_gather | solution.py:26
  17.6 0.7 gather_fusion.1
  18.3 1.0 %broadcast_select_fusion = bf16[8,18,16,128]{3,2,1,0:T(8,128)(2,1)} fusion(bf16[8,18,16,128]{3,2,1,0:T(8,128)(2,1)S(1)} %bitcast.32, pred[8,18]{1,0:T(8,128)(4,1)S(1)} %broadcast_compare_fusion), kind=kLoop, calls=%fused_computation.11 | loop fusion | flops 294912 | bytes 1179792 | tf_op jit(solution)/shard_map/jit(_where)/select_n | solution.py:37
  19.4 6.0 %all-to-all-start.1 = ((bf16[8,18,16,128]{3,2,1,0:T(8,128)(2,1)}), bf16[8,18,16,128]{3,2,1,0:T(8,128)(2,1)S(1)}, u32[]{:S(2)}, u32[]{:S(2)}) async-start(bf16[8,18,16,128]{3,2,1,0:T(8,128)(2,1)} %broadcast_select_fusion), calls=%async_computation.1 | async-start | bytes 1179648 | tf_op jit(solution)/shard_map/all_to_all | solution.py:38
  25.4 3.2 %copy.42 = bf16[24,1,128,128]{0,3,2,1:T(8,128)(2,1)} copy(bf16[24,1,128,128]{3,2,1,0:T(8,128)(2,1)S(1)} %slice-done) | data formatting | bytes 1572864
  28.6 1.9 %gather_fusion = bf16[128,24]{1,0:T(8,128)(2,1)S(1)} fusion(bf16[24,128,128]{0,2,1:T(8,128)(2,1)} %bitcast.31, s32[128]{0:T(128)S(1)} %or_bitcast_fusion), kind=kCustom, calls=%fused_computation | custom fusion | bytes 13312 | tf_op jit(solution)/shard_map/jit(diagonal)/gather | solution.py:44
  31.1 10.7 %all-to-all-done.1 = bf16[8,18,16,128]{3,2,1,0:T(8,128)(2,1)S(1)} async-done(((bf16[8,18,16,128]{3,2,1,0:T(8,128)(2,1)}), bf16[8,18,16,128]{3,2,1,0:T(8,128)(2,1)S(1)}, u32[]{:S(2)}, u32[]{:S(2)}) %all-to-all-start.1) | async-done | bytes 589856 | tf_op jit(solution)/shard_map/all_to_all | solution.py:38
  41.8 0.6 gather_fusion.2
  42.5 1.8 %gather_fusion.3 = bf16[288,16,128]{2,1,0:T(8,128)(2,1)S(1)} fusion(bf16[222,16,128]{2,1,0:T(8,128)(2,1)S(1)} %pad_maximum_fusion, s32[1024]{0:T(1024)S(1)} %pad_clamp_fusion), kind=kCustom, calls=%fused_computation.3 | custom fusion | bytes 2360448 | tf_op jit(solution)/shard_map/gather | solution.py:42
  44.4 7.5 %subtract_convert_fusion = (bf16[24,12,16,128]{3,2,1,0:T(8,128)(2,1)S(1)}, f32[24,12,16,128]{3,2,1,0:T(8,128)S(1)}) fusion(f32[24,128]{1,0:T(8,128)S(1)} %multiply_bitcast_fusion, f32[24,16,128]{2,1,0:T(8,128)S(1)} %convert_element_type.46, f32[12]{0:T(128)S(1)} %compare_convert_fusion, bf16[24,12,16,128]{3,2,1,0:T(8,128)(2,1)S(1)} %bitcast.30, ...), kind=kOutput, calls=%fused_computation.4 | convolution fusion | flops 153354240 | bytes 14364720 | tf_op jit(solution)/shard_map/tkrc,tkmc->tkmr/dot_general | solution.py:43
  51.8 2.0 %convolution_multiply_fusion = f32[24,12,16,16]{3,2,1,0:T(8,128)S(1)} fusion(bf16[24,12,16,128]{3,2,1,0:T(8,128)(2,1)S(1)} %get-tuple-element.4, f32[24,12,16,128]{3,2,1,0:T(8,128)S(1)} %get-tuple-element.5), kind=kOutput, calls=%fused_computation.5 | convolution fusion | flops 113319936 | bytes 3833856 | tf_op jit(solution)/shard_map/tkmr,tknr->tkmn/dot_general | solution.py:51
  53.8 1.7 %reshape.91 = f32[288,256]{1,0:T(8,128)} reshape(f32[24,12,16,16]{3,2,1,0:T(8,128)S(1)} %convolution_multiply_fusion) | data formatting | bytes 589824 | tf_op jit(solution)/shard_map/reshape | solution.py:56
  55.5 1.5 %fusion.2 = f32[222,256]{1,0:T(8,128)S(1)} fusion(f32[288,256]{1,0:T(8,128)} %reshape.91, s32[288]{0:T(512)S(1)} %eq.58), kind=kOutput, calls=%fused_computation.13 | convolution fusion | flops 196475328 | bytes 523392 | tf_op jit(solution)/shard_map/dot_general | solution.py:61
  57.1 0.3 convolution_convert_fusion
  57.4 0.7 copy.41
  58.0 3.6 %all-to-all-start.2 = ((bf16[8,18,256]{2,1,0:T(8,128)(2,1)}), bf16[8,18,256]{2,1,0:T(8,128)(2,1)S(1)}, u32[]{:S(2)}, u32[]{:S(2)}) async-start(bf16[8,18,256]{2,1,0:T(8,128)(2,1)} %copy.41), calls=%async_computation.2 | async-start | bytes 196608 | tf_op jit(solution)/shard_map/all_to_all | solution.py:71
  61.7 7.1 %all-to-all-done.2 = bf16[8,18,256]{2,1,0:T(8,128)(2,1)S(1)} async-done(((bf16[8,18,256]{2,1,0:T(8,128)(2,1)}), bf16[8,18,256]{2,1,0:T(8,128)(2,1)S(1)}, u32[]{:S(2)}, u32[]{:S(2)}) %all-to-all-start.2) | async-done | bytes 73760 | tf_op jit(solution)/shard_map/all_to_all | solution.py:71
  68.8 0.3 fusion.1
  69.1 5.6 %all-gather = bf16[384,256]{1,0:T(8,128)(2,1)S(1)} all-gather(bf16[96,256]{1,0:T(8,128)(2,1)S(1)} %fusion.1), channel_id=2, replica_groups=mesh['sub'=8,'blk'=4] {'blk'}, dimensions={0}, use_global_device_ids=true | all-gather | bytes 245760 | tf_op jit(solution)/shard_map/all_gather | solution.py:11
  74.7 0.6 convert_element_type.53
  (35 shorter events, 1.1 us)
Async XLA Ops:
  0.6 24.7 %copy-start.1 = (bf16[24,16,128]{2,1,0:T(8,128)(2,1)S(1)}, bf16[24,16,128]{2,1,0:T(8,128)(2,1)}, u32[]{:S(2)}) copy-start(bf16[24,16,128]{2,1,0:T(8,128)(2,1)} %param.5) | copy-start | bytes 294916
  3.5 14.0 %all-to-all-start = ((s32[8,1,18]{2,1,0:T(1,128)}), s32[8,1,18]{2,1,0:T(1,128)S(1)}, u32[]{:S(2)}, u32[]{:S(2)}) async-start(s32[8,1,18]{2,1,0:T(1,128)} %bitcast.4), calls=%async_computation | async-start | bytes 8192 | tf_op jit(solution)/shard_map/all_to_all | solution.py:34
  18.3 7.1 %slice-start = ((bf16[24,12,128,128]{3,2,1,0:T(8,128)(2,1)}), bf16[24,1,128,128]{3,2,1,0:T(8,128)(2,1)S(1)}, s32[]{:S(2)}) async-start(bf16[24,12,128,128]{3,2,1,0:T(8,128)(2,1)} %param.4), calls=%async_computation.3 | async-start | bytes 1572864 | tf_op jit(solution)/shard_map/slice | solution.py:44
  19.4 22.4 %all-to-all-start.1 = ((bf16[8,18,16,128]{3,2,1,0:T(8,128)(2,1)}), bf16[8,18,16,128]{3,2,1,0:T(8,128)(2,1)S(1)}, u32[]{:S(2)}, u32[]{:S(2)}) async-start(bf16[8,18,16,128]{3,2,1,0:T(8,128)(2,1)} %broadcast_select_fusion), calls=%async_computation.1 | async-start | bytes 1179648 | tf_op jit(solution)/shard_map/all_to_all | solution.py:38
  25.4 5.3 %copy-start.2 = (s32[24,12]{0,1:T(8,128)S(1)}, s32[24,12]{0,1:T(8,128)}, u32[]{:S(2)}) copy-start(s32[24,12]{0,1:T(8,128)} %param.6) | copy-start | bytes 3460
  51.8 2.0 %copy-start = (bf16[24,12,16,128]{3,2,1,0:T(8,128)(2,1)}, bf16[24,12,16,128]{3,2,1,0:T(8,128)(2,1)S(1)}, u32[]{:S(2)}) copy-start(bf16[24,12,16,128]{3,2,1,0:T(8,128)(2,1)S(1)} %get-tuple-element.4) | copy-start | bytes 3538948
  58.0 10.8 %all-to-all-start.2 = ((bf16[8,18,256]{2,1,0:T(8,128)(2,1)}), bf16[8,18,256]{2,1,0:T(8,128)(2,1)S(1)}, u32[]{:S(2)}, u32[]{:S(2)}) async-start(bf16[8,18,256]{2,1,0:T(8,128)(2,1)} %copy.41), calls=%async_computation.2 | async-start | bytes 196608 | tf_op jit(solution)/shard_map/all_to_all | solution.py:71
